TPU v7x, 32 devices: a whole 2x2x4 slice. The times are simulated.
32 devices in a mesh: dp: 8 (over y, x, core), tensor: 4 (over z).
Axes of the slice: x: 2, y: 2, z: 4, core: 2. Of those that a mesh axis runs over, the one named last changes fastest.
Arguments:
- tokens: bfloat16 [4096, 3072], P('dp', 'tensor'), may hold values from -6 to 6
- cotangent: bfloat16 [4096, 1024], P('dp'), may hold values from -8 to 8
- weight: bfloat16 [3072, 1024], P('tensor'), may hold values from -6 to 6
- momentum: bfloat16 [8, 3072, 1024], P('dp', 'tensor'), may hold values from -1.1953125 to 1.1953125
- threshold: int32 [1024], replicated, may hold values from 2 to 8
Outputs:
- key_values: bfloat16 [4096, 1024], P(('dp', 'tensor'))
- input_grad: bfloat16 [4096, 3072], P('dp', 'tensor')
- new_momentum: bfloat16 [8, 3072, 1024], P('dp', 'tensor')
- new_weight: bfloat16 [3072, 1024], P('tensor', 'dp')
All inputs are finite; a program needn't handle non-finite values.
Results may differ from a plain program's by a relative error of at most 0.017.
Values may be sent and summed in bfloat16 or wider, within the bound.
No kernel may reach another device: no remote copies, remote signals or barrier semaphores. Data moves between devices by JAX's collectives and lax.ppermute only.
A program may use at most 64 MiB of HBM per device.

v0:
```python
import jax
import jax.numpy as jnp
from jax import lax
from jax.sharding import PartitionSpec as P

D = 3072


def per_device(tokens, cotangent, weight, momentum, threshold):
    inverse = D ** (-0.5)
    key_values = lax.psum_scatter(
        (jnp.dot(tokens, weight, preferred_element_type=jnp.float32) * inverse).astype(
            jnp.bfloat16
        ),
        "tensor",
        scatter_dimension=0,
        tiled=True,
    )
    input_grad = (
        lax.dot_general(
            cotangent, weight, (((1,), (1,)), ((), ())), preferred_element_type=jnp.float32
        )
        * inverse
    ).astype(jnp.bfloat16)
    gradient = (
        lax.dot_general(
            tokens, cotangent, (((0,), (0,)), ((), ())), preferred_element_type=jnp.float32
        )
        * inverse
    )
    fresh = (0.9 * momentum[0].astype(jnp.float32) + 0.1 * gradient).astype(jnp.bfloat16)
    column_share = weight.shape[1] // lax.axis_size("dp")
    arrived = lax.all_to_all(fresh[None], "dp", split_axis=2, concat_axis=0, tiled=True)
    votes = jnp.sum(jnp.clip(arrived.astype(jnp.float32) / 0.125, -1.0, 1.0), axis=0)
    first_column = lax.axis_index("dp") * column_share
    own_columns = lax.dynamic_slice_in_dim(weight, first_column, column_share, 1)
    own_limits = lax.dynamic_slice_in_dim(threshold, first_column, column_share, 0)
    update = jnp.clip(votes / own_limits.astype(jnp.float32)[None, :], -1.0, 1.0)
    new_weight = (own_columns.astype(jnp.float32) - 0.5 * update).astype(jnp.bfloat16)
    return (key_values, input_grad, fresh[None], new_weight)


def solution(mesh):
    in_specs = (P("dp", "tensor"), P("dp", None), P("tensor", None), P("dp", "tensor", None), P())
    out_specs = (
        P(("dp", "tensor"), None),
        P("dp", "tensor"),
        P("dp", "tensor", None),
        P("tensor", "dp"),
    )
    return jax.shard_map(
        per_device, mesh=mesh, in_specs=in_specs, out_specs=out_specs, check_vma=False
    )
```

profile of v0, /device:TPU:0, one launch (start us, length us, event | category | flops | bytes accessed | tf_op | source)
XLA Modules:
  0.0 78.0 jit_solution(1171594350504713559)
XLA Ops:
  7.2 0.0 copy-start
  7.2 3.2 %fusion.1 = bf16[1,768,1024]{2,1,0:T(8,128)(2,1)S(1)} fusion(bf16[512,768]{1,0:T(8,128)(2,1)} %param.5, bf16[512,1024]{1,0:T(8,128)(2,1)} %param.6, bf16[1,768,1024]{2,1,0:T(8,128)(2,1)} %param.8), kind=kOutput, calls=%fused_computation.5 | convolution fusion | flops 809238528 | bytes 4980736 | tf_op jit(solution)/shard_map/dot_general | solution.py:26
  10.3 0.0 copy-start.1
  10.4 5.9 %copy.11 = bf16[1,768,1024]{1,0,2:T(2,128)(2,1)} copy(bf16[1,768,1024]{2,1,0:T(8,128)(2,1)S(1)} %fusion.1) | data formatting | bytes 3145728 | tf_op jit(solution)/shard_map/broadcast_in_dim | solution.py:40
  16.3 0.0 copy-done.1
  16.3 0.5 broadcast.25
  16.8 11.2 %reduce.3 = bf16[1024,768]{1,0:T(8,128)(2,1)S(1)} reduce(bf16[1024,1,768]{2,1,0:T(2,128)(2,1)} %bitcast.18, bf16[]{:T(256)} %broadcast.25), dimensions={1}, to_apply=%bitcast.9.reduce_sub_computation | reduce | bytes 3145730
  28.0 1.9 %reshape.25 = bf16[8,2,49152]{2,1,0:T(2,128)(2,1)} reshape(bf16[1024,768]{1,0:T(8,128)(2,1)S(1)} %reduce.3) | data formatting | bytes 3145728
  29.9 5.2 %all-to-all-start = ((bf16[8,2,49152]{2,1,0:T(2,128)(2,1)}), bf16[8,2,49152]{2,1,0:T(2,128)(2,1)S(1)}, u32[]{:S(2)}, u32[]{:S(2)}) async-start(bf16[8,2,49152]{2,1,0:T(2,128)(2,1)} %reshape.25), calls=%async_computation.1 | async-start | bytes 3145728 | tf_op jit(solution)/shard_map/all_to_all | solution.py:33
  35.1 0.2 reduce-scatter.2.cloned.1.call-start
  35.3 0.0 copy-done
  35.3 3.1 %multiply_convert_fusion = bf16[512,1024]{1,0:T(8,128)(2,1)} fusion(bf16[512,768]{1,0:T(8,128)(2,1)} %param.5, bf16[768,1024]{1,0:T(8,128)(2,1)S(1)} %copy-done), kind=kOutput, calls=%fused_computation.3 | convolution fusion | flops 806354944 | bytes 3407872 | tf_op jit(solution)/shard_map/dot_general | solution.py:12
  38.4 0.0 reduce-scatter.2.cloned.1.call-update
  38.4 0.1 constant_dynamic-slice_fusion
  38.5 0.1 copy.14
  38.7 0.8 dynamic-slice_convert_fusion
  39.4 3.1 %multiply_convert_fusion.1 = bf16[512,768]{1,0:T(8,128)(2,1)} fusion(bf16[512,1024]{1,0:T(8,128)(2,1)} %param.6, bf16[768,1024]{1,0:T(8,128)(2,1)S(1)} %copy-done), kind=kOutput, calls=%fused_computation.4 | convolution fusion | flops 806092800 | bytes 3407872 | tf_op jit(solution)/shard_map/dot_general | solution.py:20
  42.5 13.5 %all-to-all-done = bf16[8,2,49152]{2,1,0:T(2,128)(2,1)S(1)} async-done(((bf16[8,2,49152]{2,1,0:T(2,128)(2,1)}), bf16[8,2,49152]{2,1,0:T(2,128)(2,1)S(1)}, u32[]{:S(2)}, u32[]{:S(2)}) %all-to-all-start) | async-done | bytes 1572896 | tf_op jit(solution)/shard_map/all_to_all | solution.py:33
  56.1 3.9 %reshape.26 = bf16[1024,1,768]{2,1,0:T(2,128)(2,1)} reshape(bf16[8,2,49152]{2,1,0:T(2,128)(2,1)S(1)} %all-to-all-done) | data formatting | bytes 3145728
  60.0 6.2 %multiply_clamp_fusion = f32[1,768,1024]{1,0,2:T(1,128)S(1)} fusion(bf16[1024,1,768]{2,1,0:T(2,128)(2,1)} %reshape.26), kind=kLoop, calls=%fused_computation.2 | loop fusion | flops 2359296 | bytes 4718592 | tf_op jit(solution)/shard_map/jit(clip)/min | solution.py:34
  66.2 1.9 %copy.13 = f32[1,768,1024]{1,2,0:T(8,128)} copy(f32[1,768,1024]{1,0,2:T(1,128)S(1)} %multiply_clamp_fusion) | data formatting | bytes 6291456
  68.1 2.1 %reduce.2 = f32[768,128]{0,1:T(8,128)S(1)} reduce(f32[768,8,128]{0,2,1:T(8,128)} %bitcast.19, f32[]{:T(128)} %constant.30.clone.1), dimensions={1}, to_apply=%region_1.2 | reduce | flops 688128 | bytes 3538948 | tf_op jit(solution)/shard_map/reduce_sum | solution.py:34
  70.2 0.1 subtract_convert_fusion
  70.4 0.8 %copy.12 = bf16[768,128]{1,0:T(8,128)(2,1)} copy(bf16[768,128]{0,1:T(8,128)(2,1)S(1)} %subtract_convert_fusion) | data formatting | bytes 393216
  71.2 0.0 reduce-scatter.2.cloned.1.call-done
Async XLA Ops:
  7.2 28.1 %copy-start = (bf16[768,1024]{1,0:T(8,128)(2,1)S(1)}, bf16[768,1024]{1,0:T(8,128)(2,1)}, u32[]{:S(2)}) copy-start(bf16[768,1024]{1,0:T(8,128)(2,1)} %param.7) | copy-start | bytes 4718596
  10.3 5.9 %copy-start.1 = (bf16[1,768,1024]{2,1,0:T(8,128)(2,1)}, bf16[1,768,1024]{2,1,0:T(8,128)(2,1)S(1)}, u32[]{:S(2)}) copy-start(bf16[1,768,1024]{2,1,0:T(8,128)(2,1)S(1)} %fusion.1) | copy-start | bytes 4718596
  29.9 26.2 %all-to-all-start = ((bf16[8,2,49152]{2,1,0:T(2,128)(2,1)}), bf16[8,2,49152]{2,1,0:T(2,128)(2,1)S(1)}, u32[]{:S(2)}, u32[]{:S(2)}) async-start(bf16[8,2,49152]{2,1,0:T(2,128)(2,1)} %reshape.25), calls=%async_computation.1 | async-start | bytes 3145728 | tf_op jit(solution)/shard_map/all_to_all | solution.py:33
  35.1 36.1 %reduce-scatter.2.cloned.1.call-start = ((), (), s32[]{:S(2)}) async-start(), calls=%async_computation.2 | async-start | bytes 1310720 | tf_op jit(solution)/shard_map/reduce_scatter | solution.py:11
Sparse Core Ops, SparseCore 0:
  38.7 28.9 reduce-scatter.1
where the time goes:
time: 78.4 us; the launch traced here: 78 us
  other arithmetic  20.5 us (26%)
  local copies, waits for them, and re-layouts  15.1 us (19%)
  between operations  14.1 us (18%)
  waiting for transfers between devices  13.5 us (17%)
  matrix products  9.39 us (12%)
  starting transfers between devices  5.41 us (7%)
    all_to_all x1, waiting for transfers between devices, per_device(): lax.all_to_all(fresh[None], 'dp', split_axis=2, concat_axis=0, tiled=True)  13.5 us
    unnamed x1, other arithmetic  11.2 us
    unnamed x10, local copies, waits for them, and re-layouts  9.15 us
    min x1, other arithmetic, per_device(): jnp.clip(arrived.astype(jnp.float32) / 0.125, -1.0, 1.0)  6.23 us
    broadcast_in_dim x1, local copies, waits for them, and re-layouts, per_device(): return (key_values, input_grad, fresh[None], new_weight)  5.9 us
    all_to_all x1, starting transfers between devices, per_device(): lax.all_to_all(fresh[None], 'dp', split_axis=2, concat_axis=0, tiled=True)  5.2 us
    dot_general x1, matrix products, per_device(): lax.dot_general(tokens, cotangent, (((0,), (0,)), ((), ())), preferred_el...  3.16 us
    dot_general x1, matrix products, per_device(): lax.dot_general(cotangent, weight, (((1,), (1,)), ((), ())), preferred_el...  3.13 us
  transfers between devices with their start and end apart: 2, of which 1 were waited for; matrix products, arithmetic and copies ran while one was open for 29% of the time, Pallas kernels for 0%

commit v1 on v0

--- a/solution.py
+++ b/solution.py
@@ -30,7 +30,10 @@
     )
     fresh = (0.9 * momentum[0].astype(jnp.float32) + 0.1 * gradient).astype(jnp.bfloat16)
     column_share = weight.shape[1] // lax.axis_size("dp")
-    arrived = lax.all_to_all(fresh[None], "dp", split_axis=2, concat_axis=0, tiled=True)
+    here_x = fresh[None]
+    arrived = jnp.concatenate(
+        lax.all_to_all(jnp.stack(jnp.split(here_x, lax.axis_size("dp"), 2), 0), "dp", 0, 0), 0
+    )
     votes = jnp.sum(jnp.clip(arrived.astype(jnp.float32) / 0.125, -1.0, 1.0), axis=0)
     first_column = lax.axis_index("dp") * column_share
     own_columns = lax.dynamic_slice_in_dim(weight, first_column, column_share, 1)

time: 78.4 us -> 53.5 us (0.68)
  other arithmetic: 20.5 us -> 2.91 us
  local copies, waits for them, and re-layouts: 15.1 us -> 5.95 us
  waiting for transfers between devices: 13.5 us -> 16.9 us
  matrix products: 9.39 us -> 8.14 us
    unnamed x1 -> x0, other arithmetic: 11.2 us -> none
    min x1 -> x0, other arithmetic: 6.23 us -> none  [per_device(): jnp.clip(arrived.astype(jnp.float32) / 0.125, -1.0, 1.0)]
    broadcast_in_dim x1 -> x0, local copies, waits for them, and re-layouts: 5.9 us -> none  [per_device(): return (key_values, input_grad, fresh[None], new_weight)]
    unnamed x10 -> x15, local copies, waits for them, and re-layouts: 9.15 us -> 5.21 us
    all_to_all x1, waiting for transfers between devices: 13.5 us -> 16.9 us  [per_device(): lax.all_to_all(jnp.stack(jnp.split(here_x, lax.axis_size('dp'), 2), 0), '...]
    dot_general x1, matrix products: 3.16 us -> 1.09 us  [per_device(): lax.dot_general(tokens, cotangent, (((0,), (0,)), ((), ())), preferred_el...]
    reduce_sum x1, other arithmetic: 2.1 us -> 0.45 us  [per_device(): jnp.sum(jnp.clip(arrived.astype(jnp.float32) / 0.125, -1.0, 1.0), axis=0)]
    convert_element_type x1, other arithmetic: 0.14 us -> 1.7 us  [per_device(): (own_columns.astype(jnp.float32) - 0.5 * update).astype(jnp.bfloat16)]
  transfers between devices with their start and end apart: 2 -> 2, of which waited for: 1 -> 1; matrix products, arithmetic and copies ran while one was open for 29% -> 25% of each run, Pallas kernels for 0% -> 0%
where the time goes in v1:
time: 53.5 us; the launch traced here: 53.3 us
  waiting for transfers between devices  16.9 us (32%)
  between operations  14.1 us (26%)
  matrix products  8.14 us (15%)
  local copies, waits for them, and re-layouts  5.95 us (11%)
  starting transfers between devices  5.23 us (10%)
  other arithmetic  2.91 us (5%)
    all_to_all x1, waiting for transfers between devices, per_device(): lax.all_to_all(jnp.stack(jnp.split(here_x, lax.axis_size('dp'), 2), 0), '...  16.9 us
    unnamed x15, local copies, waits for them, and re-layouts  5.21 us
    all_to_all x1, starting transfers between devices, per_device(): lax.all_to_all(jnp.stack(jnp.split(here_x, lax.axis_size('dp'), 2), 0), '...  5.2 us
    dot_general x1, matrix products, per_device(): jnp.dot(tokens, weight, preferred_element_type=jnp.float32) * inverse  3.75 us
    dot_general x1, matrix products, per_device(): lax.dot_general(cotangent, weight, (((1,), (1,)), ((), ())), preferred_el...  3.31 us
    convert_element_type x1, other arithmetic, per_device(): (own_columns.astype(jnp.float32) - 0.5 * update).astype(jnp.bfloat16)  1.7 us
    dot_general x1, matrix products, per_device(): lax.dot_general(tokens, cotangent, (((0,), (0,)), ((), ())), preferred_el...  1.09 us
  transfers between devices with their start and end apart: 2, of which 1 were waited for; matrix products, arithmetic and copies ran while one was open for 25% of the time, Pallas kernels for 0%

profile of v1, /device:TPU:0, one launch (start us, length us, event | category | flops | bytes accessed | tf_op | source)
XLA Modules:
  0.0 53.3 jit_solution(5248806894293349590)
XLA Ops:
  7.2 0.0 copy-start
  7.2 0.0 copy-start.3
  7.2 0.0 copy-start.2
  7.2 0.0 reduce-scatter.2.cloned.1.call-start
  7.2 3.7 %multiply_convert_fusion = bf16[512,1024]{1,0:T(8,128)(2,1)} fusion(bf16[512,768]{1,0:T(8,128)(2,1)} %param.5, bf16[768,1024]{1,0:T(8,128)(2,1)} %param.7), kind=kOutput, calls=%fused_computation.3 | convolution fusion | flops 806354944 | bytes 3407872 | tf_op jit(solution)/shard_map/dot_general | solution.py:12
  11.0 0.0 reduce-scatter.2.cloned.1.call-update
  11.0 0.0 copy-done
  11.0 0.0 copy-done.3
  11.0 0.0 copy-done.2
  11.0 1.1 %fusion.1 = bf16[1,768,1024]{2,1,0:T(8,128)(2,1)S(1)} fusion(bf16[512,768]{1,0:T(8,128)(2,1)S(1)} %copy-done.3, bf16[512,1024]{1,0:T(8,128)(2,1)S(1)} %copy-done, bf16[1,768,1024]{2,1,0:T(8,128)(2,1)S(1)} %copy-done.2), kind=kOutput, calls=%fused_computation.5 | convolution fusion | flops 809238528 | bytes 4980736 | tf_op jit(solution)/shard_map/dot_general | solution.py:26
  12.1 0.0 copy-start.1
  12.2 0.8 %fusion.9 = bf16[8,1,768,128]{3,2,1,0:T(8,128)(2,1)} fusion(bf16[1,768,1024]{2,1,0:T(8,128)(2,1)S(1)} %fusion.1), kind=kLoop, calls=%fused_computation.22 | loop fusion | bytes 393216
  13.0 0.7 %fusion.8 = bf16[8,1,768,128]{3,2,1,0:T(8,128)(2,1)} fusion(bf16[8,1,768,128]{3,2,1,0:T(8,128)(2,1)} %fusion.9, bf16[1,768,1024]{2,1,0:T(8,128)(2,1)S(1)} %fusion.1), kind=kLoop, calls=%fused_computation.20 | loop fusion | bytes 393216
  13.7 0.7 %fusion.7 = bf16[8,1,768,128]{3,2,1,0:T(8,128)(2,1)} fusion(bf16[8,1,768,128]{3,2,1,0:T(8,128)(2,1)} %fusion.8, bf16[1,768,1024]{2,1,0:T(8,128)(2,1)S(1)} %fusion.1), kind=kLoop, calls=%fused_computation.18 | loop fusion | bytes 393216
  14.4 0.7 %fusion.6 = bf16[8,1,768,128]{3,2,1,0:T(8,128)(2,1)} fusion(bf16[8,1,768,128]{3,2,1,0:T(8,128)(2,1)} %fusion.7, bf16[1,768,1024]{2,1,0:T(8,128)(2,1)S(1)} %fusion.1), kind=kLoop, calls=%fused_computation.16 | loop fusion | bytes 393216
  15.2 0.7 %fusion.5 = bf16[8,1,768,128]{3,2,1,0:T(8,128)(2,1)} fusion(bf16[8,1,768,128]{3,2,1,0:T(8,128)(2,1)} %fusion.6, bf16[1,768,1024]{2,1,0:T(8,128)(2,1)S(1)} %fusion.1), kind=kLoop, calls=%fused_computation.14 | loop fusion | bytes 393216
  15.9 0.7 %fusion.4 = bf16[8,1,768,128]{3,2,1,0:T(8,128)(2,1)} fusion(bf16[8,1,768,128]{3,2,1,0:T(8,128)(2,1)} %fusion.5, bf16[1,768,1024]{2,1,0:T(8,128)(2,1)S(1)} %fusion.1), kind=kLoop, calls=%fused_computation.12 | loop fusion | bytes 393216
  16.6 0.7 %fusion.3 = bf16[8,1,768,128]{3,2,1,0:T(8,128)(2,1)} fusion(bf16[8,1,768,128]{3,2,1,0:T(8,128)(2,1)} %fusion.4, bf16[1,768,1024]{2,1,0:T(8,128)(2,1)S(1)} %fusion.1), kind=kLoop, calls=%fused_computation.10 | loop fusion | bytes 393216
  17.3 0.0 copy-done.1
  17.3 0.7 %fusion.2 = bf16[8,1,768,128]{3,2,1,0:T(8,128)(2,1)} fusion(bf16[8,1,768,128]{3,2,1,0:T(8,128)(2,1)} %fusion.3, bf16[1,768,1024]{2,1,0:T(8,128)(2,1)S(1)} %fusion.1), kind=kLoop, calls=%fused_computation.8 | loop fusion | bytes 393216 | tf_op jit(solution)/shard_map/stack | solution.py:35
  18.1 5.2 %all-to-all-start = ((bf16[8,1,768,128]{3,2,1,0:T(8,128)(2,1)}), bf16[8,1,768,128]{3,2,1,0:T(8,128)(2,1)S(1)}, u32[]{:S(2)}, u32[]{:S(2)}) async-start(bf16[8,1,768,128]{3,2,1,0:T(8,128)(2,1)} %fusion.2), calls=%async_computation.1 | async-start | bytes 3145728 | tf_op jit(solution)/shard_map/all_to_all | solution.py:35
  23.3 0.8 %dynamic-slice_convert_fusion = f32[128]{0:T(128)S(1)} fusion(s32[1024]{0:T(1024)} %param.9, s32[]{:T(128)S(6)} %select_n.4), kind=kLoop, calls=%fused_computation.23 | loop fusion | flops 128 | bytes 1028 | tf_op jit(solution)/shard_map/convert_element_type | solution.py:41
  24.0 3.3 %multiply_convert_fusion.1 = bf16[512,768]{1,0:T(8,128)(2,1)} fusion(bf16[512,1024]{1,0:T(8,128)(2,1)S(1)} %copy-done, bf16[768,1024]{1,0:T(8,128)(2,1)} %param.7), kind=kOutput, calls=%fused_computation.4 | convolution fusion | flops 806092800 | bytes 3407872 | tf_op jit(solution)/shard_map/dot_general | solution.py:20
  27.4 16.9 %all-to-all-done = bf16[8,1,768,128]{3,2,1,0:T(8,128)(2,1)S(1)} async-done(((bf16[8,1,768,128]{3,2,1,0:T(8,128)(2,1)}), bf16[8,1,768,128]{3,2,1,0:T(8,128)(2,1)S(1)}, u32[]{:S(2)}, u32[]{:S(2)}) %all-to-all-start) | async-done | bytes 1572896 | tf_op jit(solution)/shard_map/all_to_all | solution.py:35
  44.3 0.5 clamp_reduce_fusion
  44.7 1.7 %subtract_convert_fusion = bf16[768,128]{1,0:T(8,128)(2,1)} fusion(f32[768,128]{1,0:T(8,128)S(1)} %clamp_reduce_fusion, f32[128]{0:T(128)S(1)} %dynamic-slice_convert_fusion, bf16[768,1024]{1,0:T(8,128)(2,1)} %param.7, s32[]{:T(128)S(6)} %select_n.4), kind=kLoop, calls=%fused_computation.6 | loop fusion | flops 589824 | bytes 786948 | tf_op jit(solution)/shard_map/convert_element_type | solution.py:42
  46.4 0.0 reduce-scatter.2.cloned.1.call-done
Async XLA Ops:
  7.2 3.9 %copy-start = (bf16[512,1024]{1,0:T(8,128)(2,1)S(1)}, bf16[512,1024]{1,0:T(8,128)(2,1)}, u32[]{:S(2)}) copy-start(bf16[512,1024]{1,0:T(8,128)(2,1)} %param.6) | copy-start | bytes 3145732
  7.2 3.9 %copy-start.3 = (bf16[512,768]{1,0:T(8,128)(2,1)S(1)}, bf16[512,768]{1,0:T(8,128)(2,1)}, u32[]{:S(2)}) copy-start(bf16[512,768]{1,0:T(8,128)(2,1)} %param.5) | copy-start | bytes 2359300
  7.2 3.9 %copy-start.2 = (bf16[1,768,1024]{2,1,0:T(8,128)(2,1)S(1)}, bf16[1,768,1024]{2,1,0:T(8,128)(2,1)}, u32[]{:S(2)}) copy-start(bf16[1,768,1024]{2,1,0:T(8,128)(2,1)} %param.8) | copy-start | bytes 4718596
  7.2 39.2 %reduce-scatter.2.cloned.1.call-start = ((), (), s32[]{:S(2)}) async-start(), calls=%async_computation.2 | async-start | bytes 1310720 | tf_op jit(solution)/shard_map/reduce_scatter | solution.py:11
  12.1 5.2 %copy-start.1 = (bf16[1,768,1024]{2,1,0:T(8,128)(2,1)}, bf16[1,768,1024]{2,1,0:T(8,128)(2,1)S(1)}, u32[]{:S(2)}) copy-start(bf16[1,768,1024]{2,1,0:T(8,128)(2,1)S(1)} %fusion.1) | copy-start | bytes 4718596
  18.1 26.2 %all-to-all-start = ((bf16[8,1,768,128]{3,2,1,0:T(8,128)(2,1)}), bf16[8,1,768,128]{3,2,1,0:T(8,128)(2,1)S(1)}, u32[]{:S(2)}, u32[]{:S(2)}) async-start(bf16[8,1,768,128]{3,2,1,0:T(8,128)(2,1)} %fusion.2), calls=%async_computation.1 | async-start | bytes 3145728 | tf_op jit(solution)/shard_map/all_to_all | solution.py:35
Sparse Core Ops, SparseCore 0:
  11.1 29.9 reduce-scatter.1
